TPU v7x, 32 devices: a whole 2x2x4 slice. The times are simulated.
32 devices in a mesh: row: 8 (over z, x), col: 4 (over y, core).
Axes of the slice: x: 2, y: 2, z: 4, core: 2. Of those that a mesh axis runs over, the one named last changes fastest.
Arguments:
- patches: bfloat16 [256, 64, 768], P('row', 'col'), may hold values from -6 to 6
- norm_gain: float32 [768], replicated, may hold values from 0.25 to 1.75
- w_qkv: bfloat16 [768, 2304], replicated, may hold values from -0.21875 to 0.21875
- pool_q: float32 [9, 768], replicated, may hold values from -30 to 30, as said below
- pool_kv: float32 [9, 1536], replicated, may hold values from -2 to 2
- w_out: bfloat16 [768, 768], replicated, may hold values from -0.21875 to 0.21875
Outputs:
- mixed: bfloat16 [128, 32, 768], P('row', 'col')
Inputs may be any that keep to these rules, and one draw needn't show every extreme that they name: `pool_q`: query pooling taps, nonzero, of either sign.
All inputs are finite; a program needn't handle non-finite values.
Results may differ from a plain program's by a relative error of at most 0.017.
The roundings to bfloat16 on the way count: a program that leaves them out, or rounds other values in their place, can miss the bound.
Values may be sent and summed in bfloat16 or wider, within the bound.
A program may use at most 128 MiB of HBM per device.

v0:
```python
import functools
import math

import jax
import jax.numpy as jnp
from jax import lax
from jax.experimental import pallas as pl
from jax.experimental.pallas import tpu as pltpu
from jax.sharding import PartitionSpec as P

HEADS = 12
MESH = pl.DeviceIdType.MESH


def passed_along(block, axis, distance):
    devices = range(lax.axis_size(axis))
    route = [(i - distance, i) for i in devices if i - distance in devices]
    return lax.ppermute(block, axis, route)


def layer_norm(patches, norm_gain):
    values = patches.astype(jnp.float32)
    center = values - jnp.mean(values, axis=-1, keepdims=True)
    spread = jnp.mean(center * center, axis=-1, keepdims=True)
    return (center * lax.rsqrt(spread + 1e-06) * norm_gain).astype(jnp.bfloat16)


def pool_grid(padded, kernel, stride, out_rows, out_cols):
    summed = jnp.zeros((out_rows, out_cols, padded.shape[-1]), jnp.float32)
    for row_off in range(3):
        for col_off in range(3):
            window = padded[
                row_off : row_off + stride * out_rows : stride,
                col_off : col_off + stride * out_cols : stride,
            ]
            summed = summed + kernel[3 * row_off + col_off] * window.astype(jnp.float32)
    return summed.astype(jnp.bfloat16)


def make_step(queries, width):
    head_size = width // HEADS
    scale = float(head_size) ** (-0.5)

    def one_block(carry, block):
        run_max, run_sum, accum = carry
        count = block.shape[0]
        key_heads = block[:, :width].reshape(count, HEADS, head_size)
        val_heads = block[:, width:].reshape(count, HEADS, head_size)
        scores = (
            jnp.einsum("qhd,khd->hqk", queries, key_heads, preferred_element_type=jnp.float32)
            * scale
        )
        new_max = jnp.maximum(run_max, jnp.max(scores, axis=-1))
        factor = jnp.exp(run_max - new_max)
        expo = jnp.exp(scores - new_max[..., None])
        run_sum = run_sum * factor + jnp.sum(expo, axis=-1)
        weights = expo.astype(jnp.bfloat16)
        accum = accum * factor[..., None] + jnp.einsum(
            "hqk,khd->hqd", weights, val_heads, preferred_element_type=jnp.float32
        )
        return ((new_max, run_sum, accum), None)

    return one_block


def start_state(query_count, width):
    return (
        jnp.full((HEADS, query_count), -1e30, jnp.float32),
        jnp.zeros((HEADS, query_count), jnp.float32),
        jnp.zeros((HEADS, query_count, width // HEADS), jnp.float32),
    )


def fold_keys(carry, queries, keyvals, width):
    count = keyvals.shape[0]
    block_len = 512
    stacked = keyvals.reshape(count // block_len, block_len, keyvals.shape[1])
    carry, unused = lax.scan(make_step(queries, width), carry, stacked)
    return carry


def on_device(patches, norm_gain, w_qkv, pool_q, pool_kv, w_out):
    tile_rows, tile_cols, width = patches.shape
    head_size = width // HEADS
    normed = layer_norm(patches, norm_gain)
    projected = jnp.dot(normed.reshape(-1, width), w_qkv, preferred_element_type=jnp.float32)
    projected = projected.astype(jnp.bfloat16).reshape(tile_rows, tile_cols, 3 * width)
    upper = passed_along(projected[-1:], "row", 1)
    taller = jnp.concatenate([upper, projected], axis=0)
    left_rim = passed_along(taller[:, -1:], "col", 1)
    extended = jnp.concatenate([left_rim, taller], axis=1)
    query_flat = pool_grid(extended[..., :width], pool_q, 2, tile_rows // 2, tile_cols // 2)
    query_flat = query_flat.reshape(-1, width)
    keyvals = pool_grid(extended[..., width:], pool_kv, 4, tile_rows // 4, tile_cols // 4)
    keyvals = keyvals.reshape(-1, 2 * width)
    query_count = query_flat.shape[0]
    queries = query_flat.reshape(query_count, HEADS, head_size)
    every_key = lax.all_gather(keyvals, ("row", "col"), axis=0, tiled=True)
    carry = fold_keys(start_state(query_count, width), queries, every_key, width)
    run_max, run_sum, accum = carry
    attended = (
        (accum / run_sum[..., None])
        .transpose(1, 0, 2)
        .reshape(query_count, width)
        .astype(jnp.bfloat16)
    )
    mixed = jnp.dot(attended, w_out, preferred_element_type=jnp.float32).astype(jnp.bfloat16)
    return mixed.reshape(tile_rows // 2, tile_cols // 2, width)


def phase_lists():
    kv = [(a - 1, b - 1) for a in range(3) for b in range(3)]
    rest = [(r, c) for r in range(-1, 4) for c in range(-1, 4) if (r, c) not in kv]
    return kv, rest


def select_rows(phases, rows, cols, total, left_at, up_at, corner_at):
    kr, kc = rows // 4, cols // 4
    t = lax.broadcasted_iota(jnp.int32, (kr * kc, 1), 0)
    m = t // kc
    n = t - m * kc
    lanes = lax.broadcasted_iota(jnp.int32, (kr * kc, total), 1)
    parts = []
    for r_off, c_off in phases:
        r, c = 4 * m + r_off, 4 * n + c_off
        src = r * cols + c
        if c_off < 0:
            src = jnp.where(c < 0, left_at + r, src)
        if r_off < 0:
            src = jnp.where(r < 0, jnp.where(c < 0, corner_at, up_at + c), src)
        parts.append(jnp.where(lanes == src, 1.0, 0.0).astype(jnp.bfloat16))
    return jnp.concatenate(parts, axis=0)


def dot32(a, b):
    return jnp.dot(a, b, preferred_element_type=jnp.float32)


def section_kernel(
    nr, nc, patches, gain, w_qkv, pool_q, pool_kv, w_out, out,
    ext, col_out, col_in, row_in, cor_in, kv_out, kv_all, q_out, q_in, att_out, att_in,
    h_send, h_recv, a_send, a_recv, g_send, g_recv, q_send, q_recv, o_send, o_recv,
):
    rows, cols, width = patches.shape
    head = width // HEADS
    group = width // nc
    heads = HEADS // nc
    per = (rows // 4) * (cols // 4)
    r, c = lax.axis_index("row"), lax.axis_index("col")
    partner = r + 1 - 2 * lax.rem(r, 2)
    steps = nr // 2
    local = rows * cols
    left_at, up_at = local, local + rows
    corner_at = up_at + cols + cols - 1
    total = ext.shape[0]

    def peer(k):
        return lax.rem(c + k, nc)

    barrier = pltpu.get_barrier_semaphore()

    def greet(to):
        pl.semaphore_signal(barrier, inc=1, device_id=to, device_id_type=MESH)

    for k in range(1, nc):
        greet((r, peer(k)))
    pl.when(r > 0)(lambda: greet((r - 1, c)))
    pl.when(r < nr - 1)(lambda: greet((r + 1, c)))
    pl.when((r > 0) & (c > 0))(lambda: greet((r - 1, c - 1)))
    pl.when((r < nr - 1) & (c < nc - 1))(lambda: greet((r + 1, c + 1)))
    pl.when(r > 1)(lambda: greet((r - 2, c)))
    pl.when(r < nr - 2)(lambda: greet((r + 2, c)))

    for i in range(rows // 8):
        col_out[8 * i : 8 * i + 8] = patches[8 * i : 8 * i + 8, cols - 1, :]

    def one_if(yes):
        return jnp.where(yes, 1, 0)

    greeters = nc - 1 + one_if(r > 0) + one_if(r < nr - 1) + one_if(r > 1) + one_if(r < nr - 2)
    greeters += one_if((r > 0) & (c > 0)) + one_if((r < nr - 1) & (c < nc - 1))
    pl.semaphore_wait(barrier, greeters)

    def remote(src, dst, send, recv, to):
        return pltpu.make_async_remote_copy(
            src_ref=src, dst_ref=dst, send_sem=send, recv_sem=recv,
            device_id=to, device_id_type=MESH,
        )

    row_copy = remote(patches.at[rows - 1], row_in, h_send.at[0], h_recv.at[0], (r + 1, c))
    col_copy = remote(col_out, col_in, h_send.at[1], h_recv.at[1], (r, c + 1))
    cor_copy = remote(patches.at[rows - 1], cor_in, h_send.at[2], h_recv.at[2], (r + 1, c + 1))
    pl.when(r < nr - 1)(lambda: row_copy.start())
    pl.when(c < nc - 1)(lambda: col_copy.start())
    pl.when((r < nr - 1) & (c < nc - 1))(lambda: cor_copy.start())

    def norm(block):
        values = block.astype(jnp.float32)
        center = values - jnp.mean(values, axis=-1, keepdims=True)
        spread = jnp.mean(center * center, axis=-1, keepdims=True)
        return (center * lax.rsqrt(spread + 1e-06) * gain[...]).astype(jnp.bfloat16)

    piece = 4

    def norm_step(i, carry):
        block = patches[pl.ds(i * piece, piece)].reshape(piece * cols, width)
        at = pl.multiple_of(i * piece * cols, piece * cols)
        ext[pl.ds(at, piece * cols), :] = norm(block)
        return carry

    lax.fori_loop(0, rows // piece, norm_step, 0)

    def halo(present, copy, source, at, count):
        @pl.when(present)
        def _():
            copy.wait_recv()
            ext[at : at + count, :] = norm(source[...])

        @pl.when(jnp.logical_not(present))
        def _():
            ext[at : at + count, :] = jnp.zeros((count, width), jnp.bfloat16)

    halo(r > 0, row_copy, row_in, up_at, cols)
    halo(c > 0, col_copy, col_in, left_at, rows)
    halo((r > 0) & (c > 0), cor_copy, cor_in, up_at + cols, cols)

    kv_phases, rest = phase_lists()
    place = (rows, cols, total, left_at, up_at, corner_at)
    x_kv = dot32(select_rows(kv_phases, *place), ext[...]).astype(jnp.bfloat16)

    def pooled(values, lookup, taps, lanes, base_r, base_c):
        acc = None
        for a in range(3):
            for b in range(3):
                k = lookup[(base_r + a - 1, base_c + b - 1)]
                tap = taps[3 * a + b : 3 * a + b + 1, lanes]
                term = tap * values[k * per : (k + 1) * per].astype(jnp.float32)
                acc = term if acc is None else acc + term
        return acc.astype(jnp.bfloat16)

    kv_at = {p: i for i, p in enumerate(kv_phases)}
    for half in range(2):
        lanes = slice(half * width, (half + 1) * width)
        proj = dot32(x_kv, w_qkv[:, (1 + half) * width : (2 + half) * width]).astype(jnp.bfloat16)
        got = pooled(proj, kv_at, pool_kv, lanes, 0, 0)
        for g in range(nc):
            kv_out[g, :, half * group : (half + 1) * group] = got[:, g * group : (g + 1) * group]

    def kv_copy(k):
        to = peer(k)
        return remote(kv_out.at[to], kv_all.at[r, c], a_send.at[k], a_recv.at[k], (r, to))

    kv_copies = [kv_copy(k) for k in range(1, nc)]
    for copy in kv_copies:
        copy.start()
    kv_all[r, c] = kv_out[c]

    x_rest = dot32(select_rows(rest, *place), ext[...]).astype(jnp.bfloat16)
    x_all = jnp.concatenate([x_kv, x_rest], axis=0)
    all_at = {p: i for i, p in enumerate(kv_phases + rest)}

    for copy in kv_copies:
        copy.wait_recv()

    def relay(slot, lane, to):
        return remote(kv_all.at[slot], kv_all.at[slot], g_send.at[lane, slot], g_recv.at[slot], to)

    def send_up(slot, start):
        copy = relay(slot, 0, (r + 2, c))
        pl.when(r + 2 < nr)(lambda: copy.start() if start else copy.wait_send())

    def send_down(slot, start):
        copy = relay(slot, 1, (r - 2, c))
        pl.when(r >= 2)(lambda: copy.start() if start else copy.wait_send())

    def send_over(slot, start):
        copy = relay(slot, 2, (partner, c))
        copy.start() if start else copy.wait_send()

    def each(step, start):
        low, high = r - 2 * step, r + 2 * step

        @pl.when(low >= 0)
        def _():
            if start:
                relay(low, 0, (r, c)).wait_recv()
            send_up(low, start)
            send_over(low, start)

        @pl.when(high < nr)
        def _():
            if start:
                relay(high, 0, (r, c)).wait_recv()
            send_down(high, start)
            send_over(high, start)

    send_up(r, True)
    send_down(r, True)
    send_over(r, True)

    proj = dot32(x_all, w_qkv[:, :width]).astype(jnp.bfloat16)
    parts = [
        pooled(proj, all_at, pool_q, slice(0, width), 2 * p, 2 * q)
        for p in range(2)
        for q in range(2)
    ]
    mixed_order = jnp.concatenate(parts, axis=0)
    count = 4 * per
    t = lax.broadcasted_iota(jnp.int32, (count, 1), 0)
    q_row = t // (cols // 2)
    q_col = t - q_row * (cols // 2)
    which = 2 * lax.rem(q_row, 2) + lax.rem(q_col, 2)
    src = which * per + (q_row // 2) * (cols // 4) + q_col // 2
    lanes = lax.broadcasted_iota(jnp.int32, (count, count), 1)
    order = jnp.where(lanes == src, 1.0, 0.0).astype(jnp.bfloat16)
    natural = dot32(order, mixed_order).astype(jnp.bfloat16)
    wide = q_out.shape[2]
    for g in range(nc):
        piece_q = natural[:, g * group : (g + 1) * group]
        q_out[g] = jnp.concatenate(
            [piece_q, jnp.zeros((count, wide - group), jnp.bfloat16)], axis=1
        )

    def q_copy(k):
        to = peer(k)
        return remote(q_out.at[to], q_in.at[c], q_send.at[k], q_recv.at[k], (r, to))

    q_copies = [q_copy(k) for k in range(1, nc)]
    for copy in q_copies:
        copy.start()
    q_in[c] = q_out[c]

    for step in range(1, steps):
        each(step, True)
    for copy in q_copies:
        copy.wait_recv()
    for k in range(steps):
        slot = 2 * k + 1 - lax.rem(r, 2)
        relay(slot, 2, (partner, c)).wait_recv()

    keys = nr * nc * per
    factor = float(head) ** (-0.5) * math.log2(math.e)
    kv_lanes = 2 * group

    def attend(g):
        q = q_in[g]
        lane = lax.broadcasted_iota(jnp.int32, (count, wide), 1)
        stacked = jnp.concatenate(
            [
                jnp.where((lane >= h * head) & (lane < (h + 1) * head), q, jnp.zeros_like(q))
                for h in range(heads)
            ],
            axis=0,
        )
        k_part = kv_all[:, :, :, 0:wide].reshape(keys, wide)
        scores = lax.dot_general(
            stacked, k_part, (((1,), (1,)), ((), ())), preferred_element_type=jnp.float32
        )
        top = jnp.max(scores, axis=-1, keepdims=True)
        expo = jnp.exp2((scores - top) * factor)
        summed = jnp.sum(expo, axis=-1, keepdims=True)
        v_part = kv_all[:, :, :, kv_lanes - wide : kv_lanes].reshape(keys, wide)
        numer = dot32(expo.astype(jnp.bfloat16), v_part) / summed
        shift = wide - group
        result = jnp.zeros((count, wide), jnp.float32)
        for h in range(heads):
            inside = (lane >= shift + h * head) & (lane < shift + (h + 1) * head)
            result = jnp.where(inside, numer[h * count : (h + 1) * count], result)
        att_out[g] = result.astype(jnp.bfloat16)

    def att_copy(k):
        to = peer(k)
        return remote(att_out.at[to], att_in.at[c], o_send.at[k], o_recv.at[k], (r, to))

    att_copies = [att_copy(k) for k in range(1, nc)]

    def attend_step(k, carry):
        attend(peer(k + 1))
        return carry

    lax.fori_loop(0, nc - 1, attend_step, 0)
    for copy in att_copies:
        copy.start()
    attend(c)
    att_in[c] = att_out[c]
    for copy in att_copies:
        copy.wait_recv()
    attended = jnp.concatenate([att_in[g][:, wide - group :] for g in range(nc)], axis=1)
    out[...] = dot32(attended, w_out[...]).astype(jnp.bfloat16)

    pl.when(r < nr - 1)(lambda: row_copy.wait_send())
    pl.when(c < nc - 1)(lambda: col_copy.wait_send())
    pl.when((r < nr - 1) & (c < nc - 1))(lambda: cor_copy.wait_send())
    for copy in kv_copies + q_copies + att_copies:
        copy.wait_send()
    send_up(r, False)
    send_down(r, False)
    send_over(r, False)
    for step in range(1, steps):
        each(step, False)


def by_kernel(nr, nc, patches, norm_gain, w_qkv, pool_q, pool_kv, w_out):
    rows, cols, width = patches.shape
    per = (rows // 4) * (cols // 4)
    count = 4 * per
    group = width // nc
    wide = -(-group // 128) * 128
    total = rows * cols + rows + 2 * cols
    total = -(-total // 16) * 16
    bf16 = jnp.bfloat16
    dma = pltpu.SemaphoreType.DMA
    vmem = pl.BlockSpec(memory_space=pltpu.VMEM)
    mixed = pl.pallas_call(
        functools.partial(section_kernel, nr, nc),
        out_shape=jax.ShapeDtypeStruct((count, width), bf16),
        in_specs=[vmem] * 6,
        out_specs=vmem,
        scratch_shapes=[
            pltpu.VMEM((total, width), bf16),
            pltpu.VMEM((rows, width), bf16),
            pltpu.VMEM((rows, width), bf16),
            pltpu.VMEM((cols, width), bf16),
            pltpu.VMEM((cols, width), bf16),
            pltpu.VMEM((nc, per, 2 * group), bf16),
            pltpu.VMEM((nr, nc, per, 2 * group), bf16),
            pltpu.VMEM((nc, count, wide), bf16),
            pltpu.VMEM((nc, count, wide), bf16),
            pltpu.VMEM((nc, count, wide), bf16),
            pltpu.VMEM((nc, count, wide), bf16),
            dma((3,)), dma((3,)),
            dma((nc,)), dma((nc,)),
            dma((3, nr)), dma((nr,)),
            dma((nc,)), dma((nc,)),
            dma((nc,)), dma((nc,)),
        ],
        compiler_params=pltpu.CompilerParams(
            collective_id=0, has_side_effects=True, vmem_limit_bytes=56 * 1024 * 1024
        ),
    )(patches, norm_gain.reshape(1, width), w_qkv, pool_q, pool_kv, w_out)
    return mixed.reshape(rows // 2, cols // 2, width)


def solution(mesh):
    nr, nc = mesh.shape["row"], mesh.shape["col"]
    placed = (P("row", "col", None), P(), P(), P(), P(), P())
    fits = nr % 2 == 0 and HEADS % nc == 0
    body = functools.partial(by_kernel, nr, nc) if fits else on_device
    return jax.shard_map(
        body, mesh=mesh, in_specs=placed, out_specs=P("row", "col", None), check_vma=False
    )
```

profile of v0, /device:TPU:0, one launch (start us, length us, event | category | flops | bytes accessed | tf_op | source)
XLA Modules:
  0.0 41.6 jit_solution(18354869760317554861)
XLA Ops:
  0.0 1.3 %reshape.6.gain = f32[1,768]{1,0:T(1,128)} reshape(f32[768]{0:T(1024)} %param.7) | data formatting | bytes 6144 | tf_op jit(solution)/shard_map/reshape | solution.py:440
  1.3 38.7 %shard_map.64 = bf16[128,768]{1,0:T(8,128)(2,1)} custom-call(bf16[32,16,768]{2,1,0:T(8,128)(2,1)} %patches.1, f32[1,768]{1,0:T(1,128)} %reshape.6.gain, bf16[768,2304]{1,0:T(8,128)(2,1)} %w_qkv.1, f32[9,768]{1,0:T(8,128)} %pool_q.1, f32[9,1536]{1,0:T(8,128)} %pool_kv.1, bf16[768,768]{1,0:T(8,128)(2,1)} %w_out.1), custom_call_target="tpu_custom_call" | custom-call | tf_op jit(solution)/shard_map/pallas_call | solution.py:414
  40.0 1.6 %copy.8 = bf16[16,8,768]{2,1,0:T(8,128)(2,1)} copy(bf16[16,8,768]{2,1,0:T(8,128)(2,1)} %bitcast.1) | data formatting | bytes 393216
where the time goes:
time: 41.8 us; the launch traced here: 41.6 us
  Pallas kernels  38.7 us (93%)
  local copies, waits for them, and re-layouts  2.88 us (7%)
    pallas_call x1, Pallas kernels, by_kernel(): pl.pallas_call(functools.partial(section_kernel, nr, nc), out_shape=jax.S...  38.7 us
    unnamed x1, local copies, waits for them, and re-layouts  1.62 us
    reshape x1, local copies, waits for them, and re-layouts, by_kernel(): norm_gain.reshape(1, width)  1.27 us

commit v1 on v0

v1 whole, which is shorter than its diff:
```python
import functools
import math

import jax
import jax.numpy as jnp
from jax import lax
from jax.experimental import pallas as pl
from jax.experimental.pallas import tpu as pltpu
from jax.sharding import PartitionSpec as P

HEADS = 12
MESH = pl.DeviceIdType.MESH


def passed_along(block, axis, distance):
    devices = range(lax.axis_size(axis))
    route = [(i - distance, i) for i in devices if i - distance in devices]
    return lax.ppermute(block, axis, route)


def layer_norm(patches, norm_gain):
    values = patches.astype(jnp.float32)
    center = values - jnp.mean(values, axis=-1, keepdims=True)
    spread = jnp.mean(center * center, axis=-1, keepdims=True)
    return (center * lax.rsqrt(spread + 1e-06) * norm_gain).astype(jnp.bfloat16)


def pool_grid(padded, kernel, stride, out_rows, out_cols):
    summed = jnp.zeros((out_rows, out_cols, padded.shape[-1]), jnp.float32)
    for row_off in range(3):
        for col_off in range(3):
            window = padded[
                row_off : row_off + stride * out_rows : stride,
                col_off : col_off + stride * out_cols : stride,
            ]
            summed = summed + kernel[3 * row_off + col_off] * window.astype(jnp.float32)
    return summed.astype(jnp.bfloat16)


def make_step(queries, width):
    head_size = width // HEADS
    scale = float(head_size) ** (-0.5)

    def one_block(carry, block):
        run_max, run_sum, accum = carry
        count = block.shape[0]
        key_heads = block[:, :width].reshape(count, HEADS, head_size)
        val_heads = block[:, width:].reshape(count, HEADS, head_size)
        scores = (
            jnp.einsum("qhd,khd->hqk", queries, key_heads, preferred_element_type=jnp.float32)
            * scale
        )
        new_max = jnp.maximum(run_max, jnp.max(scores, axis=-1))
        factor = jnp.exp(run_max - new_max)
        expo = jnp.exp(scores - new_max[..., None])
        run_sum = run_sum * factor + jnp.sum(expo, axis=-1)
        weights = expo.astype(jnp.bfloat16)
        accum = accum * factor[..., None] + jnp.einsum(
            "hqk,khd->hqd", weights, val_heads, preferred_element_type=jnp.float32
        )
        return ((new_max, run_sum, accum), None)

    return one_block


def start_state(query_count, width):
    return (
        jnp.full((HEADS, query_count), -1e30, jnp.float32),
        jnp.zeros((HEADS, query_count), jnp.float32),
        jnp.zeros((HEADS, query_count, width // HEADS), jnp.float32),
    )


def fold_keys(carry, queries, keyvals, width):
    count = keyvals.shape[0]
    block_len = 512
    stacked = keyvals.reshape(count // block_len, block_len, keyvals.shape[1])
    carry, unused = lax.scan(make_step(queries, width), carry, stacked)
    return carry


def on_device(patches, norm_gain, w_qkv, pool_q, pool_kv, w_out):
    tile_rows, tile_cols, width = patches.shape
    head_size = width // HEADS
    normed = layer_norm(patches, norm_gain)
    projected = jnp.dot(normed.reshape(-1, width), w_qkv, preferred_element_type=jnp.float32)
    projected = projected.astype(jnp.bfloat16).reshape(tile_rows, tile_cols, 3 * width)
    upper = passed_along(projected[-1:], "row", 1)
    taller = jnp.concatenate([upper, projected], axis=0)
    left_rim = passed_along(taller[:, -1:], "col", 1)
    extended = jnp.concatenate([left_rim, taller], axis=1)
    query_flat = pool_grid(extended[..., :width], pool_q, 2, tile_rows // 2, tile_cols // 2)
    query_flat = query_flat.reshape(-1, width)
    keyvals = pool_grid(extended[..., width:], pool_kv, 4, tile_rows // 4, tile_cols // 4)
    keyvals = keyvals.reshape(-1, 2 * width)
    query_count = query_flat.shape[0]
    queries = query_flat.reshape(query_count, HEADS, head_size)
    every_key = lax.all_gather(keyvals, ("row", "col"), axis=0, tiled=True)
    carry = fold_keys(start_state(query_count, width), queries, every_key, width)
    run_max, run_sum, accum = carry
    attended = (
        (accum / run_sum[..., None])
        .transpose(1, 0, 2)
        .reshape(query_count, width)
        .astype(jnp.bfloat16)
    )
    mixed = jnp.dot(attended, w_out, preferred_element_type=jnp.float32).astype(jnp.bfloat16)
    return mixed.reshape(tile_rows // 2, tile_cols // 2, width)


def phase_lists():
    kv_local = [(r, c) for r in range(2) for c in range(2)]
    local = kv_local + [(r, c) for r in range(4) for c in range(4) if (r, c) not in kv_local]
    kv_halo = [(a, b) for a in range(-1, 2) for b in range(-1, 2) if min(a, b) < 0]
    grid = [(r, c) for r in range(-1, 4) for c in range(-1, 4) if min(r, c) < 0]
    halo = kv_halo + [p for p in grid if p not in kv_halo]
    return local, halo, len(kv_local), len(kv_halo)


def select_rows(phases, rows, cols, total, left_at, up_at, corner_at):
    kr, kc = rows // 4, cols // 4
    t = lax.broadcasted_iota(jnp.int32, (kr * kc, 1), 0)
    m = t // kc
    n = t - m * kc
    lanes = lax.broadcasted_iota(jnp.int32, (kr * kc, total), 1)
    parts = []
    for r_off, c_off in phases:
        r, c = 4 * m + r_off, 4 * n + c_off
        src = r * cols + c
        if c_off < 0:
            src = jnp.where(c < 0, left_at + r, src)
        if r_off < 0:
            src = jnp.where(r < 0, jnp.where(c < 0, corner_at, up_at + c), src)
        parts.append(jnp.where(lanes == src, 1.0, 0.0).astype(jnp.bfloat16))
    return jnp.concatenate(parts, axis=0)


def dot32(a, b):
    return jnp.dot(a, b, preferred_element_type=jnp.float32)


def section_kernel(
    nr, nc, patches, gain, w_hbm, pool_q, pool_kv, out,
    ext, col_out, col_in, row_in, cor_in, kv_out, kv_all, q_out, q_in, att_out, att_in,
    w_qkv, acc, peak, summed,
    w_sem, h_send, h_recv, a_send, a_recv, g_send, g_recv, q_send, q_recv, o_send, o_recv,
):
    rows, cols, width = patches.shape
    head = width // HEADS
    group = width // nc
    heads = HEADS // nc
    per = (rows // 4) * (cols // 4)
    r, c = lax.axis_index("row"), lax.axis_index("col")
    side, z = lax.rem(r, 2), r // 2
    core, chip = lax.rem(c, 2), c // 2
    partner = r + 1 - 2 * side
    steps, pairs = nr // 2, nc // 2
    local = rows * cols
    left_at, up_at = local, local + rows
    corner_at = up_at + cols + cols - 1
    total = ext.shape[0]

    w_copies = [
        pltpu.make_async_copy(
            w_hbm.at[:, i * width : (i + 1) * width],
            w_qkv.at[:, i * width : (i + 1) * width],
            w_sem.at[i],
        )
        for i in range(3)
    ]
    for copy in w_copies:
        copy.start()

    def peer(j):
        return 2 * lax.rem(chip + 1 + j // 2, pairs) + lax.rem(core + 1 + j, 2)

    peers = [peer(j) for j in range(nc - 1)]
    barrier = pltpu.get_barrier_semaphore()

    def greet(to):
        pl.semaphore_signal(barrier, inc=1, device_id=to, device_id_type=MESH)

    for to in peers:
        greet((r, to))
    pl.when(r > 0)(lambda: greet((r - 1, c)))
    pl.when(r < nr - 1)(lambda: greet((r + 1, c)))
    pl.when((r > 0) & (c > 0))(lambda: greet((r - 1, c - 1)))
    pl.when((r < nr - 1) & (c < nc - 1))(lambda: greet((r + 1, c + 1)))
    pl.when(r > 1)(lambda: greet((r - 2, c)))
    pl.when(r < nr - 2)(lambda: greet((r + 2, c)))

    for i in range(rows // 8):
        col_out[8 * i : 8 * i + 8] = patches[8 * i : 8 * i + 8, cols - 1, :]

    weight = gain[...].reshape(1, width)

    def norm(block):
        values = block.astype(jnp.float32)
        center = values - jnp.mean(values, axis=-1, keepdims=True)
        spread = jnp.mean(center * center, axis=-1, keepdims=True)
        return (center * lax.rsqrt(spread + 1e-06) * weight).astype(jnp.bfloat16)

    piece = 4

    def norm_step(i, carry):
        block = patches[pl.ds(i * piece, piece)].reshape(piece * cols, width)
        at = pl.multiple_of(i * piece * cols, piece * cols)
        ext[pl.ds(at, piece * cols), :] = norm(block)
        return carry

    early = rows // piece // 2
    lax.fori_loop(0, early, norm_step, 0)

    def one_if(yes):
        return jnp.where(yes, 1, 0)

    greeters = nc - 1 + one_if(r > 0) + one_if(r < nr - 1) + one_if(r > 1) + one_if(r < nr - 2)
    greeters += one_if((r > 0) & (c > 0)) + one_if((r < nr - 1) & (c < nc - 1))
    pl.semaphore_wait(barrier, greeters)

    def remote(src, dst, send, recv, to):
        return pltpu.make_async_remote_copy(
            src_ref=src, dst_ref=dst, send_sem=send, recv_sem=recv,
            device_id=to, device_id_type=MESH,
        )

    row_copy = remote(patches.at[rows - 1], row_in, h_send.at[0], h_recv.at[0], (r + 1, c))
    col_copy = remote(col_out, col_in, h_send.at[1], h_recv.at[1], (r, c + 1))
    cor_copy = remote(patches.at[rows - 1], cor_in, h_send.at[2], h_recv.at[2], (r + 1, c + 1))
    pl.when((r < nr - 1) & (c < nc - 1))(lambda: cor_copy.start())
    pl.when(r < nr - 1)(lambda: row_copy.start())
    pl.when(c < nc - 1)(lambda: col_copy.start())

    lax.fori_loop(early, rows // piece, norm_step, 0)

    local_phases, halo_phases, n_kv_local, n_kv_halo = phase_lists()
    place = (rows, cols)
    marks = (left_at, up_at, corner_at)
    x_local = dot32(select_rows(local_phases, *place, local, *marks), ext[0:local, :])
    x_local = x_local.astype(jnp.bfloat16)

    def project(x, part):
        lanes = slice(part * width, (part + 1) * width)
        return dot32(x, w_qkv[:, lanes]).astype(jnp.bfloat16)

    w_copies[0].wait()
    q_proj = {0: project(x_local, 0)}
    w_copies[1].wait()
    w_copies[2].wait()
    kv_proj = {(0, half): project(x_local[: n_kv_local * per], 1 + half) for half in range(2)}

    def halo(present, copy, source, at, count):
        @pl.when(present)
        def _():
            copy.wait_recv()
            ext[at : at + count, :] = norm(source[...])

        @pl.when(jnp.logical_not(present))
        def _():
            ext[at : at + count, :] = jnp.zeros((count, width), jnp.bfloat16)

    halo(r > 0, row_copy, row_in, up_at, cols)
    halo(c > 0, col_copy, col_in, left_at, rows)
    halo((r > 0) & (c > 0), cor_copy, cor_in, up_at + cols, cols)

    x_halo = dot32(select_rows(halo_phases, *place, total, *marks), ext[...])
    x_halo = x_halo.astype(jnp.bfloat16)
    for half in range(2):
        kv_proj[1, half] = project(x_halo[: n_kv_halo * per], 1 + half)

    found = {p: (0, i) for i, p in enumerate(local_phases)}
    found.update({p: (1, i) for i, p in enumerate(halo_phases)})

    def pooled(values, taps, lanes, base_r, base_c):
        total_term = None
        for a in range(3):
            for b in range(3):
                which, k = found[base_r + a - 1, base_c + b - 1]
                tap = taps[3 * a + b : 3 * a + b + 1, lanes]
                term = tap * values[which][k * per : (k + 1) * per].astype(jnp.float32)
                total_term = term if total_term is None else total_term + term
        return total_term.astype(jnp.bfloat16)

    for half in range(2):
        lanes = slice(half * width, (half + 1) * width)
        got = pooled({w: kv_proj[w, half] for w in range(2)}, pool_kv, lanes, 0, 0)
        for g in range(nc):
            kv_out[g, :, half * group : (half + 1) * group] = got[:, g * group : (g + 1) * group]

    def kv_copy(j, to):
        mine = kv_all.at[side, z, chip, core]
        return remote(kv_out.at[to], mine, a_send.at[j], a_recv.at[c], (r, to))

    def kv_wait(j, to):
        slot = kv_all.at[side, z, to // 2, lax.rem(to, 2)]
        remote(kv_out.at[to], slot, a_send.at[j], a_recv.at[to], (r, to)).wait_recv()

    kv_copies = [kv_copy(j, to) for j, to in enumerate(peers)]
    for copy in kv_copies:
        copy.start()
    kv_all[side, z, chip, core] = kv_out[c]

    def relay(level, pair, lane, to):
        slot = kv_all.at[side, level, pair]
        return remote(slot, slot, g_send.at[lane, level, pair], g_recv.at[side, level, pair], to)

    def send_along(level, pair, lane, start):
        to_row = (r + 2, r - 2, partner)[lane]
        copy = relay(level, pair, lane, (to_row, c))

        def act():
            copy.start() if start else copy.wait_send()

        if lane == 0:
            pl.when(z + 1 < steps)(act)
        elif lane == 1:
            pl.when(z >= 1)(act)
        else:
            act()

    def chunk(j):
        return lax.rem(chip + j, pairs)

    def own(j, start):
        for lane in range(3):
            send_along(z, chunk(j), lane, start)

    def each(step, j, start):
        for level, there, lane in ((z - step, z - step >= 0, 0), (z + step, z + step < steps, 1)):

            @pl.when(there)
            def _():
                if start:
                    relay(level, chunk(j), lane, (partner, c)).wait_recv()
                send_along(level, chunk(j), lane, start)
                send_along(level, chunk(j), 2, start)

    q_proj[1] = project(x_halo, 0)
    kv_wait(nc - 2, peers[nc - 2])
    own(0, True)

    parts = [
        pooled(q_proj, pool_q, slice(0, width), 2 * p, 2 * q) for p in range(2) for q in range(2)
    ]
    mixed_order = jnp.concatenate(parts, axis=0)
    count = 4 * per
    t = lax.broadcasted_iota(jnp.int32, (count, 1), 0)
    q_row = t // (cols // 2)
    q_col = t - q_row * (cols // 2)
    which = 2 * lax.rem(q_row, 2) + lax.rem(q_col, 2)
    src = which * per + (q_row // 2) * (cols // 4) + q_col // 2
    lanes = lax.broadcasted_iota(jnp.int32, (count, count), 1)
    order = jnp.where(lanes == src, 1.0, 0.0).astype(jnp.bfloat16)
    natural = dot32(order, mixed_order).astype(jnp.bfloat16)
    wide = q_out.shape[2]
    for g in range(nc):
        piece_q = natural[:, g * group : (g + 1) * group]
        q_out[g] = jnp.concatenate(
            [piece_q, jnp.zeros((count, wide - group), jnp.bfloat16)], axis=1
        )

    def q_copy(j, to):
        return remote(q_out.at[to], q_in.at[c], q_send.at[j], q_recv.at[c], (r, to))

    q_copies = [q_copy(j, to) for j, to in enumerate(peers)]
    for copy in q_copies:
        copy.start()
    q_in[c] = q_out[c]

    for j in range(nc - 2):
        kv_wait(j, peers[j])
    for j in range(1, pairs):
        own(j, True)
    for step in range(1, steps):
        for j in range(pairs):
            each(step, j, True)
    for j, to in enumerate(peers):
        remote(q_out.at[to], q_in.at[to], q_send.at[j], q_recv.at[to], (r, to)).wait_recv()

    keys = steps * nc * per
    factor = float(head) ** (-0.5) * math.log2(math.e)
    kv_lanes = 2 * group
    lane = lax.broadcasted_iota(jnp.int32, (count, wide), 1)
    shift = wide - group

    def scores_of(g, from_side):
        q = q_in[g]
        stacked = jnp.concatenate(
            [
                jnp.where((lane >= h * head) & (lane < (h + 1) * head), q, jnp.zeros_like(q))
                for h in range(heads)
            ],
            axis=0,
        )
        k_part = kv_all[from_side, :, :, :, :, 0:wide].reshape(keys, wide)
        return lax.dot_general(
            stacked, k_part, (((1,), (1,)), ((), ())), preferred_element_type=jnp.float32
        )

    def weighted(expo, from_side):
        v_part = kv_all[from_side, :, :, :, :, kv_lanes - wide : kv_lanes].reshape(keys, wide)
        return dot32(expo.astype(jnp.bfloat16), v_part)

    def first_half(g, carry):
        scores = scores_of(g, side)
        top = jnp.max(scores, axis=-1, keepdims=True)
        expo = jnp.exp2((scores - top) * factor)
        peak[g] = top
        summed[g] = jnp.sum(expo, axis=-1, keepdims=True)
        acc[g] = weighted(expo, side)
        return carry

    lax.fori_loop(0, nc, first_half, 0)

    for level in range(steps):
        for pair in range(pairs):
            slot = kv_all.at[1 - side, level, pair]
            remote(
                slot, slot, g_send.at[2, level, pair], g_recv.at[1 - side, level, pair],
                (partner, c),
            ).wait_recv()

    def second_half(g):
        scores = scores_of(g, 1 - side)
        before = peak[g]
        top = jnp.maximum(before, jnp.max(scores, axis=-1, keepdims=True))
        expo = jnp.exp2((scores - top) * factor)
        fade = jnp.exp2((before - top) * factor)
        whole = summed[g] * fade + jnp.sum(expo, axis=-1, keepdims=True)
        numer = (acc[g] * fade + weighted(expo, 1 - side)) / whole
        result = jnp.zeros((count, wide), jnp.float32)
        for h in range(heads):
            inside = (lane >= shift + h * head) & (lane < shift + (h + 1) * head)
            result = jnp.where(inside, numer[h * count : (h + 1) * count], result)
        result = result[:, shift:].astype(jnp.bfloat16)
        half = count // 2
        att_out[g] = jnp.concatenate([result[:half], result[half:]], axis=1)

    def att_copy(j, to):
        return remote(att_out.at[to], att_in.at[c], o_send.at[j], o_recv.at[c], (r, to))

    def second_step(j, carry):
        to = peer(j)
        second_half(to)
        att_copy(j, to).start()
        return carry

    lax.fori_loop(0, nc - 1, second_step, 0)
    second_half(c)
    att_in[c] = att_out[c]
    for j, to in enumerate(peers):
        remote(att_out.at[to], att_in.at[to], o_send.at[j], o_recv.at[to], (r, to)).wait_recv()
    half = count // 2
    out[:half] = jnp.concatenate([att_in[g][:, :group] for g in range(nc)], axis=1)
    out[half:] = jnp.concatenate([att_in[g][:, group:] for g in range(nc)], axis=1)

    pl.when(r < nr - 1)(lambda: row_copy.wait_send())
    pl.when(c < nc - 1)(lambda: col_copy.wait_send())
    pl.when((r < nr - 1) & (c < nc - 1))(lambda: cor_copy.wait_send())
    for copy in kv_copies + q_copies:
        copy.wait_send()
    for j, to in enumerate(peers):
        att_copy(j, to).wait_send()
    for j in range(pairs):
        own(j, False)
    for step in range(1, steps):
        for j in range(pairs):
            each(step, j, False)


def by_kernel(nr, nc, patches, norm_gain, w_qkv, pool_q, pool_kv, w_out):
    rows, cols, width = patches.shape
    per = (rows // 4) * (cols // 4)
    count = 4 * per
    group = width // nc
    heads = HEADS // nc
    wide = -(-group // 128) * 128
    total = rows * cols + rows + 2 * cols
    total = -(-total // 16) * 16
    steps, pairs = nr // 2, nc // 2
    bf16, f32 = jnp.bfloat16, jnp.float32
    dma = pltpu.SemaphoreType.DMA
    vmem = pl.BlockSpec(memory_space=pltpu.VMEM)
    attended = pl.pallas_call(
        functools.partial(section_kernel, nr, nc),
        out_shape=jax.ShapeDtypeStruct((count, width), bf16),
        in_specs=[vmem, vmem, pl.BlockSpec(memory_space=pl.ANY), vmem, vmem],
        out_specs=vmem,
        scratch_shapes=[
            pltpu.VMEM((total, width), bf16),
            pltpu.VMEM((rows, width), bf16),
            pltpu.VMEM((rows, width), bf16),
            pltpu.VMEM((cols, width), bf16),
            pltpu.VMEM((cols, width), bf16),
            pltpu.VMEM((nc, per, 2 * group), bf16),
            pltpu.VMEM((2, steps, pairs, 2, per, 2 * group), bf16),
            pltpu.VMEM((nc, count, wide), bf16),
            pltpu.VMEM((nc, count, wide), bf16),
            pltpu.VMEM((nc, count // 2, 2 * group), bf16),
            pltpu.VMEM((nc, count // 2, 2 * group), bf16),
            pltpu.VMEM(w_qkv.shape, bf16),
            pltpu.VMEM((nc, heads * count, wide), f32),
            pltpu.VMEM((nc, heads * count, 1), f32),
            pltpu.VMEM((nc, heads * count, 1), f32),
            dma((3,)),
            dma((3,)), dma((3,)),
            dma((nc,)), dma((nc,)),
            dma((3, steps, pairs)), dma((2, steps, pairs)),
            dma((nc,)), dma((nc,)),
            dma((nc,)), dma((nc,)),
        ],
        compiler_params=pltpu.CompilerParams(
            collective_id=0, has_side_effects=True, vmem_limit_bytes=56 * 1024 * 1024
        ),
    )(patches, norm_gain, w_qkv, pool_q, pool_kv)
    mixed = jnp.dot(attended, w_out, preferred_element_type=f32).astype(bf16)
    return mixed.reshape(rows // 2, cols // 2, width)


def solution(mesh):
    nr, nc = mesh.shape["row"], mesh.shape["col"]
    placed = (P("row", "col", None), P(), P(), P(), P(), P())
    fits = nr % 2 == 0 and nc % 2 == 0 and HEADS % nc == 0
    body = functools.partial(by_kernel, nr, nc) if fits else on_device
    return jax.shard_map(
        body, mesh=mesh, in_specs=placed, out_specs=P("row", "col", None), check_vma=False
    )
```

time: 41.8 us -> 35.5 us (0.85)
  Pallas kernels: 38.7 us -> 33.4 us
  local copies, waits for them, and re-layouts: 2.88 us -> 0.01 us
  matrix products: 0 us -> 1.93 us
    pallas_call x1, Pallas kernels: 38.7 us -> 33.4 us  [by_kernel(): pl.pallas_call(functools.partial(section_kernel, nr, nc), out_shape=jax.S...]
    dot_general x0 -> x1, matrix products: none -> 1.93 us  [by_kernel(): mixed = jnp.dot(attended, w_out, preferred_element_type=f32).astype(bf16)]
    unnamed x1 -> x2, local copies, waits for them, and re-layouts: 1.62 us -> 0.01 us
    reshape x1 -> x0, local copies, waits for them, and re-layouts: 1.27 us -> none  [by_kernel(): norm_gain.reshape(1, width)]
where the time goes in v1:
time: 35.5 us; the launch traced here: 35.4 us
  Pallas kernels  33.4 us (94%)
  matrix products  1.93 us (5%)
    pallas_call x1, Pallas kernels, by_kernel(): pl.pallas_call(functools.partial(section_kernel, nr, nc), out_shape=jax.S...  33.4 us
    dot_general x1, matrix products, by_kernel(): mixed = jnp.dot(attended, w_out, preferred_element_type=f32).astype(bf16)  1.93 us

profile of v1, /device:TPU:0, one launch (start us, length us, event | category | flops | bytes accessed | tf_op | source)
XLA Modules:
  0.0 35.4 jit_solution(784389204297543667)
XLA Ops:
  0.0 0.0 copy-start
  0.0 33.4 %shard_map.64 = bf16[128,768]{1,0:T(8,128)(2,1)} custom-call(bf16[32,16,768]{2,1,0:T(8,128)(2,1)} %patches.1, f32[768]{0:T(1024)} %gain.1, bf16[768,2304]{1,0:T(8,128)(2,1)} %w_hbm.1, f32[9,768]{1,0:T(8,128)} %pool_q.1, f32[9,1536]{1,0:T(8,128)} %pool_kv.1), custom_call_target="tpu_custom_call" | custom-call | tf_op jit(solution)/shard_map/pallas_call | solution.py:484
  33.4 0.0 copy-done
  33.4 1.9 %fusion = bf16[16,8,768]{2,1,0:T(8,128)(2,1)} fusion(bf16[128,768]{1,0:T(8,128)(2,1)} %shard_map.64, bf16[768,768]{1,0:T(8,128)(2,1)S(1)} %copy-done), kind=kOutput, calls=%fused_computation.1 | convolution fusion | flops 151093248 | bytes 1572864 | tf_op jit(solution)/shard_map/dot_general | solution.py:516
Async XLA Ops:
  0.0 33.4 %copy-start = (bf16[768,768]{1,0:T(8,128)(2,1)S(1)}, bf16[768,768]{1,0:T(8,128)(2,1)}, u32[]{:S(2)}) copy-start(bf16[768,768]{1,0:T(8,128)(2,1)} %param.11) | copy-start | bytes 3538948

commit v2 on v1

--- a/solution.py
+++ b/solution.py
@@ -142,7 +142,7 @@
 def section_kernel(
     nr, nc, patches, gain, w_hbm, pool_q, pool_kv, out,
     ext, col_out, col_in, row_in, cor_in, kv_out, kv_all, q_out, q_in, att_out, att_in,
-    w_qkv, acc, peak, summed,
+    w_qkv, q_all, acc, peak, summed,
     w_sem, h_send, h_recv, a_send, a_recv, g_send, g_recv, q_send, q_recv, o_send, o_recv,
 ):
     rows, cols, width = patches.shape
@@ -209,7 +209,7 @@
         return carry
 
     early = rows // piece // 2
-    lax.fori_loop(0, early, norm_step, 0)
+    lax.fori_loop(0, early, norm_step, 0, unroll=True)
 
     def one_if(yes):
         return jnp.where(yes, 1, 0)
@@ -231,7 +231,7 @@
     pl.when(r < nr - 1)(lambda: row_copy.start())
     pl.when(c < nc - 1)(lambda: col_copy.start())
 
-    lax.fori_loop(early, rows // piece, norm_step, 0)
+    lax.fori_loop(early, rows // piece, norm_step, 0, unroll=True)
 
     local_phases, halo_phases, n_kv_local, n_kv_halo = phase_lists()
     place = (rows, cols)
@@ -371,63 +371,84 @@
         kv_wait(j, peers[j])
     for j in range(1, pairs):
         own(j, True)
-    for step in range(1, steps):
-        for j in range(pairs):
-            each(step, j, True)
-    for j, to in enumerate(peers):
-        remote(q_out.at[to], q_in.at[to], q_send.at[j], q_recv.at[to], (r, to)).wait_recv()
-
-    keys = steps * nc * per
+    keys = nc * per
     factor = float(head) ** (-0.5) * math.log2(math.e)
     kv_lanes = 2 * group
     lane = lax.broadcasted_iota(jnp.int32, (count, wide), 1)
     shift = wide - group
-
-    def scores_of(g, from_side):
-        q = q_in[g]
-        stacked = jnp.concatenate(
-            [
-                jnp.where((lane >= h * head) & (lane < (h + 1) * head), q, jnp.zeros_like(q))
-                for h in range(heads)
-            ],
-            axis=0,
+    stack = heads * count
+
+    def stack_queries():
+        for j, to in enumerate(peers):
+            remote(q_out.at[to], q_in.at[to], q_send.at[j], q_recv.at[to], (r, to)).wait_recv()
+        for g in range(nc):
+            q = q_in[g]
+            for h in range(heads):
+                kept = (lane >= h * head) & (lane < (h + 1) * head)
+                at = g * stack + h * count
+                q_all[at : at + count, :] = jnp.where(kept, q, jnp.zeros_like(q))
+
+    def absorb(from_side, level, first=False):
+        k_part = kv_all[from_side, level, :, :, :, 0:wide].reshape(keys, wide)
+        v_part = kv_all[from_side, level, :, :, :, kv_lanes - wide : kv_lanes].reshape(keys, wide)
+        scores = lax.dot_general(
+            q_all[...], k_part, (((1,), (1,)), ((), ())), preferred_element_type=jnp.float32
         )
-        k_part = kv_all[from_side, :, :, :, :, 0:wide].reshape(keys, wide)
-        return lax.dot_general(
-            stacked, k_part, (((1,), (1,)), ((), ())), preferred_element_type=jnp.float32
-        )
-
-    def weighted(expo, from_side):
-        v_part = kv_all[from_side, :, :, :, :, kv_lanes - wide : kv_lanes].reshape(keys, wide)
-        return dot32(expo.astype(jnp.bfloat16), v_part)
-
-    def first_half(g, carry):
-        scores = scores_of(g, side)
-        top = jnp.max(scores, axis=-1, keepdims=True)
+        high = jnp.max(scores, axis=-1, keepdims=True)
+        top = high if first else jnp.maximum(peak[...], high)
         expo = jnp.exp2((scores - top) * factor)
-        peak[g] = top
-        summed[g] = jnp.sum(expo, axis=-1, keepdims=True)
-        acc[g] = weighted(expo, side)
+        piece_sum = jnp.sum(expo, axis=-1, keepdims=True)
+        numer = dot32(expo.astype(jnp.bfloat16), v_part)
+        if first:
+            summed[...] = piece_sum
+            acc[...] = numer
+        else:
+            fade = jnp.exp2((peak[...] - top) * factor)
+            summed[...] = summed[...] * fade + piece_sum
+            acc[...] = acc[...] * fade + numer
+        peak[...] = top
+
+    def absorb_both(step, visit):
+        def one(k, carry):
+            level = z - step + 2 * k * step
+            pl.when((level >= 0) & (level < steps))(lambda: visit(level))
+            return carry
+
+        lax.fori_loop(0, 2, one, 0)
+
+    for j in range(pairs):
+        each(1, j, True)
+    stack_queries()
+    absorb(side, z, True)
+
+    def own_step(step, carry):
+        absorb_both(step, lambda level: absorb(side, level))
+        for j in range(pairs):
+            each(step + 1, j, True)
         return carry
 
-    lax.fori_loop(0, nc, first_half, 0)
-
-    for level in range(steps):
+    lax.fori_loop(1, steps, own_step, 0)
+
+    def from_partner(level):
         for pair in range(pairs):
             slot = kv_all.at[1 - side, level, pair]
             remote(
                 slot, slot, g_send.at[2, level, pair], g_recv.at[1 - side, level, pair],
                 (partner, c),
             ).wait_recv()
-
-    def second_half(g):
-        scores = scores_of(g, 1 - side)
-        before = peak[g]
-        top = jnp.maximum(before, jnp.max(scores, axis=-1, keepdims=True))
-        expo = jnp.exp2((scores - top) * factor)
-        fade = jnp.exp2((before - top) * factor)
-        whole = summed[g] * fade + jnp.sum(expo, axis=-1, keepdims=True)
-        numer = (acc[g] * fade + weighted(expo, 1 - side)) / whole
+        absorb(1 - side, level)
+
+    def partner_step(k, carry):
+        step = (k + 1) // 2
+        level = z + step * (2 * lax.rem(k, 2) - 1)
+        pl.when((level >= 0) & (level < steps))(lambda: from_partner(level))
+        return carry
+
+    lax.fori_loop(0, 2 * steps - 1, partner_step, 0)
+
+    def finish(g):
+        rows_g = pl.ds(pl.multiple_of(g * stack, stack), stack)
+        numer = acc[rows_g, :] / summed[rows_g, :]
         result = jnp.zeros((count, wide), jnp.float32)
         for h in range(heads):
             inside = (lane >= shift + h * head) & (lane < shift + (h + 1) * head)
@@ -441,12 +462,12 @@
 
     def second_step(j, carry):
         to = peer(j)
-        second_half(to)
+        finish(to)
         att_copy(j, to).start()
         return carry
 
     lax.fori_loop(0, nc - 1, second_step, 0)
-    second_half(c)
+    finish(c)
     att_in[c] = att_out[c]
     for j, to in enumerate(peers):
         remote(att_out.at[to], att_in.at[to], o_send.at[j], o_recv.at[to], (r, to)).wait_recv()
@@ -499,9 +520,10 @@
             pltpu.VMEM((nc, count // 2, 2 * group), bf16),
             pltpu.VMEM((nc, count // 2, 2 * group), bf16),
             pltpu.VMEM(w_qkv.shape, bf16),
-            pltpu.VMEM((nc, heads * count, wide), f32),
-            pltpu.VMEM((nc, heads * count, 1), f32),
-            pltpu.VMEM((nc, heads * count, 1), f32),
+            pltpu.VMEM((nc * heads * count, wide), bf16),
+            pltpu.VMEM((nc * heads * count, wide), f32),
+            pltpu.VMEM((nc * heads * count, 1), f32),
+            pltpu.VMEM((nc * heads * count, 1), f32),
             dma((3,)),
             dma((3,)), dma((3,)),
             dma((nc,)), dma((nc,)),

time: 35.5 us -> 55.5 us (1.56)
  Pallas kernels: 33.4 us -> 53.4 us
    pallas_call x1, Pallas kernels: 33.4 us -> 53.4 us  [by_kernel(): pl.pallas_call(functools.partial(section_kernel, nr, nc), out_shape=jax.S...]
where the time goes in v2:
time: 55.5 us; the launch traced here: 55.3 us
  Pallas kernels  53.4 us (96%)
  matrix products  1.93 us (3%)
    pallas_call x1, Pallas kernels, by_kernel(): pl.pallas_call(functools.partial(section_kernel, nr, nc), out_shape=jax.S...  53.4 us
    dot_general x1, matrix products, by_kernel(): mixed = jnp.dot(attended, w_out, preferred_element_type=f32).astype(bf16)  1.93 us

profile of v2, /device:TPU:0, one launch (start us, length us, event | category | flops | bytes accessed | tf_op | source)
XLA Modules:
  0.0 55.3 jit_solution(9316565642443871181)
XLA Ops:
  0.0 0.0 copy-start
  0.0 53.4 %shard_map.64 = bf16[128,768]{1,0:T(8,128)(2,1)} custom-call(bf16[32,16,768]{2,1,0:T(8,128)(2,1)} %patches.1, f32[768]{0:T(1024)} %gain.1, bf16[768,2304]{1,0:T(8,128)(2,1)} %w_hbm.1, f32[9,768]{1,0:T(8,128)} %pool_q.1, f32[9,1536]{1,0:T(8,128)} %pool_kv.1), custom_call_target="tpu_custom_call" | custom-call | tf_op jit(solution)/shard_map/pallas_call | solution.py:505
  53.4 0.0 copy-done
  53.4 1.9 %fusion = bf16[16,8,768]{2,1,0:T(8,128)(2,1)} fusion(bf16[128,768]{1,0:T(8,128)(2,1)} %shard_map.64, bf16[768,768]{1,0:T(8,128)(2,1)S(1)} %copy-done), kind=kOutput, calls=%fused_computation.1 | convolution fusion | flops 151093248 | bytes 1572864 | tf_op jit(solution)/shard_map/dot_general | solution.py:538
Async XLA Ops:
  0.0 53.4 %copy-start = (bf16[768,768]{1,0:T(8,128)(2,1)S(1)}, bf16[768,768]{1,0:T(8,128)(2,1)}, u32[]{:S(2)}) copy-start(bf16[768,768]{1,0:T(8,128)(2,1)} %param.11) | copy-start | bytes 3538948

commit v3 on v1

--- a/solution.py
+++ b/solution.py
@@ -142,7 +142,7 @@
 def section_kernel(
     nr, nc, patches, gain, w_hbm, pool_q, pool_kv, out,
     ext, col_out, col_in, row_in, cor_in, kv_out, kv_all, q_out, q_in, att_out, att_in,
-    w_qkv, acc, peak, summed,
+    w_qkv, v_turned, acc, peak, summed,
     w_sem, h_send, h_recv, a_send, a_recv, g_send, g_recv, q_send, q_recv, o_send, o_recv,
 ):
     rows, cols, width = patches.shape
@@ -209,7 +209,7 @@
         return carry
 
     early = rows // piece // 2
-    lax.fori_loop(0, early, norm_step, 0)
+    lax.fori_loop(0, early, norm_step, 0, unroll=True)
 
     def one_if(yes):
         return jnp.where(yes, 1, 0)
@@ -231,7 +231,7 @@
     pl.when(r < nr - 1)(lambda: row_copy.start())
     pl.when(c < nc - 1)(lambda: col_copy.start())
 
-    lax.fori_loop(early, rows // piece, norm_step, 0)
+    lax.fori_loop(early, rows // piece, norm_step, 0, unroll=True)
 
     local_phases, halo_phases, n_kv_local, n_kv_halo = phase_lists()
     place = (rows, cols)
@@ -394,20 +394,25 @@
         )
         k_part = kv_all[from_side, :, :, :, :, 0:wide].reshape(keys, wide)
         return lax.dot_general(
-            stacked, k_part, (((1,), (1,)), ((), ())), preferred_element_type=jnp.float32
-        )
-
-    def weighted(expo, from_side):
+            k_part, stacked, (((1,), (1,)), ((), ())), preferred_element_type=jnp.float32
+        )
+
+    def turn_values(from_side):
         v_part = kv_all[from_side, :, :, :, :, kv_lanes - wide : kv_lanes].reshape(keys, wide)
-        return dot32(expo.astype(jnp.bfloat16), v_part)
+        v_turned[...] = v_part.T[shift:, :]
+
+    def weighted(expo):
+        return dot32(v_turned[...], expo.astype(jnp.bfloat16))
+
+    turn_values(side)
 
     def first_half(g, carry):
         scores = scores_of(g, side)
-        top = jnp.max(scores, axis=-1, keepdims=True)
+        top = jnp.max(scores, axis=0, keepdims=True)
         expo = jnp.exp2((scores - top) * factor)
         peak[g] = top
-        summed[g] = jnp.sum(expo, axis=-1, keepdims=True)
-        acc[g] = weighted(expo, side)
+        summed[g] = jnp.sum(expo, axis=0, keepdims=True)
+        acc[g] = weighted(expo)
         return carry
 
     lax.fori_loop(0, nc, first_half, 0)
@@ -423,18 +428,17 @@
     def second_half(g):
         scores = scores_of(g, 1 - side)
         before = peak[g]
-        top = jnp.maximum(before, jnp.max(scores, axis=-1, keepdims=True))
+        top = jnp.maximum(before, jnp.max(scores, axis=0, keepdims=True))
         expo = jnp.exp2((scores - top) * factor)
         fade = jnp.exp2((before - top) * factor)
-        whole = summed[g] * fade + jnp.sum(expo, axis=-1, keepdims=True)
-        numer = (acc[g] * fade + weighted(expo, 1 - side)) / whole
-        result = jnp.zeros((count, wide), jnp.float32)
-        for h in range(heads):
-            inside = (lane >= shift + h * head) & (lane < shift + (h + 1) * head)
-            result = jnp.where(inside, numer[h * count : (h + 1) * count], result)
-        result = result[:, shift:].astype(jnp.bfloat16)
-        half = count // 2
-        att_out[g] = jnp.concatenate([result[:half], result[half:]], axis=1)
+        whole = summed[g] * fade + jnp.sum(expo, axis=0, keepdims=True)
+        numer = (acc[g] * fade + weighted(expo)) / whole
+        picked = [
+            numer[h * head : (h + 1) * head, h * count : (h + 1) * count] for h in range(heads)
+        ]
+        att_out[g] = jnp.concatenate(picked, axis=0).astype(jnp.bfloat16)
+
+    turn_values(1 - side)
 
     def att_copy(j, to):
         return remote(att_out.at[to], att_in.at[c], o_send.at[j], o_recv.at[c], (r, to))
@@ -450,9 +454,8 @@
     att_in[c] = att_out[c]
     for j, to in enumerate(peers):
         remote(att_out.at[to], att_in.at[to], o_send.at[j], o_recv.at[to], (r, to)).wait_recv()
-    half = count // 2
-    out[:half] = jnp.concatenate([att_in[g][:, :group] for g in range(nc)], axis=1)
-    out[half:] = jnp.concatenate([att_in[g][:, group:] for g in range(nc)], axis=1)
+    for g in range(nc):
+        out[g * group : (g + 1) * group, :] = att_in[g]
 
     pl.when(r < nr - 1)(lambda: row_copy.wait_send())
     pl.when(c < nc - 1)(lambda: col_copy.wait_send())
@@ -483,7 +486,7 @@
     vmem = pl.BlockSpec(memory_space=pltpu.VMEM)
     attended = pl.pallas_call(
         functools.partial(section_kernel, nr, nc),
-        out_shape=jax.ShapeDtypeStruct((count, width), bf16),
+        out_shape=jax.ShapeDtypeStruct((width, count), bf16),
         in_specs=[vmem, vmem, pl.BlockSpec(memory_space=pl.ANY), vmem, vmem],
         out_specs=vmem,
         scratch_shapes=[
@@ -496,12 +499,13 @@
             pltpu.VMEM((2, steps, pairs, 2, per, 2 * group), bf16),
             pltpu.VMEM((nc, count, wide), bf16),
             pltpu.VMEM((nc, count, wide), bf16),
-            pltpu.VMEM((nc, count // 2, 2 * group), bf16),
-            pltpu.VMEM((nc, count // 2, 2 * group), bf16),
+            pltpu.VMEM((nc, group, count), bf16),
+            pltpu.VMEM((nc, group, count), bf16),
             pltpu.VMEM(w_qkv.shape, bf16),
-            pltpu.VMEM((nc, heads * count, wide), f32),
-            pltpu.VMEM((nc, heads * count, 1), f32),
-            pltpu.VMEM((nc, heads * count, 1), f32),
+            pltpu.VMEM((group, steps * nc * per), bf16),
+            pltpu.VMEM((nc, group, heads * count), f32),
+            pltpu.VMEM((nc, 1, heads * count), f32),
+            pltpu.VMEM((nc, 1, heads * count), f32),
             dma((3,)),
             dma((3,)), dma((3,)),
             dma((nc,)), dma((nc,)),
@@ -513,7 +517,9 @@
             collective_id=0, has_side_effects=True, vmem_limit_bytes=56 * 1024 * 1024
         ),
     )(patches, norm_gain, w_qkv, pool_q, pool_kv)
-    mixed = jnp.dot(attended, w_out, preferred_element_type=f32).astype(bf16)
+    mixed = lax.dot_general(
+        attended, w_out, (((0,), (0,)), ((), ())), preferred_element_type=f32
+    ).astype(bf16)
     return mixed.reshape(rows // 2, cols // 2, width)
 
 

time: 35.5 us -> 34.7 us (0.977)
  Pallas kernels: 33.4 us -> 32.5 us
    pallas_call x1, Pallas kernels: 33.4 us -> 32.5 us  [by_kernel(): pl.pallas_call(functools.partial(section_kernel, nr, nc), out_shape=jax.S...]
where the time goes in v3:
time: 34.7 us; the launch traced here: 34.5 us
  Pallas kernels  32.5 us (94%)
  matrix products  1.96 us (6%)
    pallas_call x1, Pallas kernels, by_kernel(): pl.pallas_call(functools.partial(section_kernel, nr, nc), out_shape=jax.S...  32.5 us
    dot_general x1, matrix products, by_kernel(): lax.dot_general(attended, w_out, (((0,), (0,)), ((), ())), preferred_elem...  1.96 us

profile of v3, /device:TPU:0, one launch (start us, length us, event | category | flops | bytes accessed | tf_op | source)
XLA Modules:
  0.0 34.5 jit_solution(8003596700854478699)
XLA Ops:
  0.0 0.0 copy-start
  0.0 32.5 %shard_map.64 = bf16[768,128]{1,0:T(8,128)(2,1)} custom-call(bf16[32,16,768]{2,1,0:T(8,128)(2,1)} %patches.1, f32[768]{0:T(1024)} %gain.1, bf16[768,2304]{1,0:T(8,128)(2,1)} %w_hbm.1, f32[9,768]{1,0:T(8,128)} %pool_q.1, f32[9,1536]{1,0:T(8,128)} %pool_kv.1), custom_call_target="tpu_custom_call" | custom-call | tf_op jit(solution)/shard_map/pallas_call | solution.py:487
  32.5 0.0 copy-done
  32.5 2.0 %fusion = bf16[16,8,768]{2,1,0:T(8,128)(2,1)} fusion(bf16[768,128]{1,0:T(8,128)(2,1)} %shard_map.64, bf16[768,768]{1,0:T(8,128)(2,1)S(1)} %copy-done), kind=kOutput, calls=%fused_computation.1 | convolution fusion | flops 151093248 | bytes 1572864 | tf_op jit(solution)/shard_map/dot_general | solution.py:520
Async XLA Ops:
  0.0 32.5 %copy-start = (bf16[768,768]{1,0:T(8,128)(2,1)S(1)}, bf16[768,768]{1,0:T(8,128)(2,1)}, u32[]{:S(2)}) copy-start(bf16[768,768]{1,0:T(8,128)(2,1)} %param.11) | copy-start | bytes 3538948

commit v4 on v2

--- a/solution.py
+++ b/solution.py
@@ -392,13 +392,13 @@
         k_part = kv_all[from_side, level, :, :, :, 0:wide].reshape(keys, wide)
         v_part = kv_all[from_side, level, :, :, :, kv_lanes - wide : kv_lanes].reshape(keys, wide)
         scores = lax.dot_general(
-            q_all[...], k_part, (((1,), (1,)), ((), ())), preferred_element_type=jnp.float32
+            k_part, q_all[...], (((1,), (1,)), ((), ())), preferred_element_type=jnp.float32
         )
-        high = jnp.max(scores, axis=-1, keepdims=True)
+        high = jnp.max(scores, axis=0, keepdims=True)
         top = high if first else jnp.maximum(peak[...], high)
         expo = jnp.exp2((scores - top) * factor)
-        piece_sum = jnp.sum(expo, axis=-1, keepdims=True)
-        numer = dot32(expo.astype(jnp.bfloat16), v_part)
+        piece_sum = jnp.sum(expo, axis=0, keepdims=True)
+        numer = dot32(v_part.T[shift:, :], expo.astype(jnp.bfloat16))
         if first:
             summed[...] = piece_sum
             acc[...] = numer
@@ -447,15 +447,12 @@
     lax.fori_loop(0, 2 * steps - 1, partner_step, 0)
 
     def finish(g):
-        rows_g = pl.ds(pl.multiple_of(g * stack, stack), stack)
-        numer = acc[rows_g, :] / summed[rows_g, :]
-        result = jnp.zeros((count, wide), jnp.float32)
-        for h in range(heads):
-            inside = (lane >= shift + h * head) & (lane < shift + (h + 1) * head)
-            result = jnp.where(inside, numer[h * count : (h + 1) * count], result)
-        result = result[:, shift:].astype(jnp.bfloat16)
-        half = count // 2
-        att_out[g] = jnp.concatenate([result[:half], result[half:]], axis=1)
+        lanes_g = pl.ds(pl.multiple_of(g * stack, 128), stack)
+        numer = acc[:, lanes_g] / summed[:, lanes_g]
+        picked = [
+            numer[h * head : (h + 1) * head, h * count : (h + 1) * count] for h in range(heads)
+        ]
+        att_out[g] = jnp.concatenate(picked, axis=0).astype(jnp.bfloat16)
 
     def att_copy(j, to):
         return remote(att_out.at[to], att_in.at[c], o_send.at[j], o_recv.at[c], (r, to))
@@ -471,9 +468,8 @@
     att_in[c] = att_out[c]
     for j, to in enumerate(peers):
         remote(att_out.at[to], att_in.at[to], o_send.at[j], o_recv.at[to], (r, to)).wait_recv()
-    half = count // 2
-    out[:half] = jnp.concatenate([att_in[g][:, :group] for g in range(nc)], axis=1)
-    out[half:] = jnp.concatenate([att_in[g][:, group:] for g in range(nc)], axis=1)
+    for g in range(nc):
+        out[g * group : (g + 1) * group, :] = att_in[g]
 
     pl.when(r < nr - 1)(lambda: row_copy.wait_send())
     pl.when(c < nc - 1)(lambda: col_copy.wait_send())
@@ -504,7 +500,7 @@
     vmem = pl.BlockSpec(memory_space=pltpu.VMEM)
     attended = pl.pallas_call(
         functools.partial(section_kernel, nr, nc),
-        out_shape=jax.ShapeDtypeStruct((count, width), bf16),
+        out_shape=jax.ShapeDtypeStruct((width, count), bf16),
         in_specs=[vmem, vmem, pl.BlockSpec(memory_space=pl.ANY), vmem, vmem],
         out_specs=vmem,
         scratch_shapes=[
@@ -517,13 +513,13 @@
             pltpu.VMEM((2, steps, pairs, 2, per, 2 * group), bf16),
             pltpu.VMEM((nc, count, wide), bf16),
             pltpu.VMEM((nc, count, wide), bf16),
-            pltpu.VMEM((nc, count // 2, 2 * group), bf16),
-            pltpu.VMEM((nc, count // 2, 2 * group), bf16),
+            pltpu.VMEM((nc, group, count), bf16),
+            pltpu.VMEM((nc, group, count), bf16),
             pltpu.VMEM(w_qkv.shape, bf16),
             pltpu.VMEM((nc * heads * count, wide), bf16),
-            pltpu.VMEM((nc * heads * count, wide), f32),
-            pltpu.VMEM((nc * heads * count, 1), f32),
-            pltpu.VMEM((nc * heads * count, 1), f32),
+            pltpu.VMEM((group, nc * heads * count), f32),
+            pltpu.VMEM((1, nc * heads * count), f32),
+            pltpu.VMEM((1, nc * heads * count), f32),
             dma((3,)),
             dma((3,)), dma((3,)),
             dma((nc,)), dma((nc,)),
@@ -535,7 +531,9 @@
             collective_id=0, has_side_effects=True, vmem_limit_bytes=56 * 1024 * 1024
         ),
     )(patches, norm_gain, w_qkv, pool_q, pool_kv)
-    mixed = jnp.dot(attended, w_out, preferred_element_type=f32).astype(bf16)
+    mixed = lax.dot_general(
+        attended, w_out, (((0,), (0,)), ((), ())), preferred_element_type=f32
+    ).astype(bf16)
     return mixed.reshape(rows // 2, cols // 2, width)
 
 

time: 55.5 us -> 34.5 us (0.62)
  Pallas kernels: 53.4 us -> 32.3 us
    pallas_call x1, Pallas kernels: 53.4 us -> 32.3 us  [by_kernel(): pl.pallas_call(functools.partial(section_kernel, nr, nc), out_shape=jax.S...]
where the time goes in v4:
time: 34.5 us; the launch traced here: 34.3 us
  Pallas kernels  32.3 us (94%)
  matrix products  1.96 us (6%)
    pallas_call x1, Pallas kernels, by_kernel(): pl.pallas_call(functools.partial(section_kernel, nr, nc), out_shape=jax.S...  32.3 us
    dot_general x1, matrix products, by_kernel(): lax.dot_general(attended, w_out, (((0,), (0,)), ((), ())), preferred_elem...  1.96 us

profile of v4, /device:TPU:0, one launch (start us, length us, event | category | flops | bytes accessed | tf_op | source)
XLA Modules:
  0.0 34.3 jit_solution(4114395381383940137)
XLA Ops:
  0.0 0.0 copy-start
  0.0 32.3 %shard_map.64 = bf16[768,128]{1,0:T(8,128)(2,1)} custom-call(bf16[32,16,768]{2,1,0:T(8,128)(2,1)} %patches.1, f32[768]{0:T(1024)} %gain.1, bf16[768,2304]{1,0:T(8,128)(2,1)} %w_hbm.1, f32[9,768]{1,0:T(8,128)} %pool_q.1, f32[9,1536]{1,0:T(8,128)} %pool_kv.1), custom_call_target="tpu_custom_call" | custom-call | tf_op jit(solution)/shard_map/pallas_call | solution.py:501
  32.3 0.0 copy-done
  32.3 2.0 %fusion = bf16[16,8,768]{2,1,0:T(8,128)(2,1)} fusion(bf16[768,128]{1,0:T(8,128)(2,1)} %shard_map.64, bf16[768,768]{1,0:T(8,128)(2,1)S(1)} %copy-done), kind=kOutput, calls=%fused_computation.1 | convolution fusion | flops 151093248 | bytes 1572864 | tf_op jit(solution)/shard_map/dot_general | solution.py:534
Async XLA Ops:
  0.0 32.3 %copy-start = (bf16[768,768]{1,0:T(8,128)(2,1)S(1)}, bf16[768,768]{1,0:T(8,128)(2,1)}, u32[]{:S(2)}) copy-start(bf16[768,768]{1,0:T(8,128)(2,1)} %param.11) | copy-start | bytes 3538948

commit v5 on v4

--- a/solution.py
+++ b/solution.py
@@ -483,6 +483,13 @@
     for step in range(1, steps):
         for j in range(pairs):
             each(step, j, False)
+
+
+def mix_kernel(attended, w_out, out):
+    mixed = lax.dot_general(
+        attended[...], w_out[...], (((0,), (0,)), ((), ())), preferred_element_type=jnp.float32
+    )
+    out[...] = mixed.astype(jnp.bfloat16)
 
 
 def by_kernel(nr, nc, patches, norm_gain, w_qkv, pool_q, pool_kv, w_out):
@@ -531,9 +538,13 @@
             collective_id=0, has_side_effects=True, vmem_limit_bytes=56 * 1024 * 1024
         ),
     )(patches, norm_gain, w_qkv, pool_q, pool_kv)
-    mixed = lax.dot_general(
-        attended, w_out, (((0,), (0,)), ((), ())), preferred_element_type=f32
-    ).astype(bf16)
+    mixed = pl.pallas_call(
+        mix_kernel,
+        out_shape=jax.ShapeDtypeStruct((count, width), bf16),
+        in_specs=[vmem, vmem],
+        out_specs=vmem,
+        compiler_params=pltpu.CompilerParams(vmem_limit_bytes=8 * 1024 * 1024),
+    )(attended, w_out)
     return mixed.reshape(rows // 2, cols // 2, width)
 
 

time: 34.5 us -> 34.4 us (level)
  matrix products: 1.96 us -> 0 us
  Pallas kernels: 32.3 us -> 33.3 us
  local copies, waits for them, and re-layouts: 0.01 us -> 0.92 us
    dot_general x1 -> x0, matrix products: 1.96 us -> none  [by_kernel(): lax.dot_general(attended, w_out, (((0,), (0,)), ((), ())), preferred_elem...]
    pallas_call x0 -> x1, Pallas kernels: none -> 1.03 us  [by_kernel(): pl.pallas_call(mix_kernel, out_shape=jax.ShapeDtypeStruct((count, width),...]
    unnamed x2 -> x4, local copies, waits for them, and re-layouts: 0.01 us -> 0.92 us
where the time goes in v5:
time: 34.4 us; the launch traced here: 34.3 us
  Pallas kernels  33.3 us (97%)
  local copies, waits for them, and re-layouts  0.92 us (3%)
    pallas_call x1, Pallas kernels, by_kernel(): pl.pallas_call(functools.partial(section_kernel, nr, nc), out_shape=jax.S...  32.3 us
    pallas_call x1, Pallas kernels, by_kernel(): pl.pallas_call(mix_kernel, out_shape=jax.ShapeDtypeStruct((count, width),...  1.03 us
    unnamed x4, local copies, waits for them, and re-layouts  0.92 us

profile of v5, /device:TPU:0, one launch (start us, length us, event | category | flops | bytes accessed | tf_op | source)
XLA Modules:
  0.0 34.3 jit_solution(8918424659834944089)
XLA Ops:
  0.0 0.0 copy-start
  0.0 32.3 %shard_map.64.attended = bf16[768,128]{1,0:T(8,128)(2,1)} custom-call(bf16[32,16,768]{2,1,0:T(8,128)(2,1)} %patches.1, f32[768]{0:T(1024)} %gain.1, bf16[768,2304]{1,0:T(8,128)(2,1)} %w_hbm.1, f32[9,768]{1,0:T(8,128)} %pool_q.1, f32[9,1536]{1,0:T(8,128)} %pool_kv.1), custom_call_target="tpu_custom_call" | custom-call | tf_op jit(solution)/shard_map/pallas_call | solution.py:508
  32.3 0.0 copy-done
  32.3 0.0 copy-start.1
  32.3 0.9 %copy-done.1 = bf16[768,128]{1,0:T(8,128)(2,1)S(1)} copy-done((bf16[768,128]{1,0:T(8,128)(2,1)S(1)}, bf16[768,128]{1,0:T(8,128)(2,1)}, u32[]{:S(2)}) %copy-start.1) | copy-done | bytes 196632
  33.3 1.0 %shard_map.65 = bf16[128,768]{1,0:T(8,128)(2,1)} custom-call(bf16[768,128]{1,0:T(8,128)(2,1)S(1)} %copy-done.1, bf16[768,768]{1,0:T(8,128)(2,1)S(1)} %copy-done), custom_call_target="tpu_custom_call" | custom-call | tf_op jit(solution)/shard_map/pallas_call | solution.py:541
Async XLA Ops:
  0.0 32.3 %copy-start = (bf16[768,768]{1,0:T(8,128)(2,1)S(1)}, bf16[768,768]{1,0:T(8,128)(2,1)}, u32[]{:S(2)}) copy-start(bf16[768,768]{1,0:T(8,128)(2,1)} %w_out.1) | copy-start | bytes 3538948
  32.3 0.9 %copy-start.1 = (bf16[768,128]{1,0:T(8,128)(2,1)S(1)}, bf16[768,128]{1,0:T(8,128)(2,1)}, u32[]{:S(2)}) copy-start(bf16[768,128]{1,0:T(8,128)(2,1)} %shard_map.64.attended) | copy-start | bytes 589828
